TPU v7x, 256 devices: a whole 4x4x8 slice. The times are simulated.
256 devices in a mesh: ctx: 32 (over x, y, core), head: 8 (over z).
Axes of the slice: x: 4, y: 4, z: 8, core: 2. Of those that a mesh axis runs over, the one named last changes fastest.
Arguments:
- queries: bfloat16 [8192, 8192], P('ctx', 'head'), may hold values from -110 to 110
- keys: bfloat16 [8192, 1024], P('ctx', 'head'), may hold values from -3.1 to 3.1
- values: bfloat16 [8192, 1024], P('ctx', 'head'), may hold values from -6 to 6
- cf_queries: bfloat16 [8192, 8192], P('ctx', 'head'), may hold values from -6 to 6
- cf_keys: bfloat16 [8192, 1024], P('ctx', 'head'), may hold values from -6 to 6
- cf_values: bfloat16 [8192, 1024], P('ctx', 'head'), may hold values from -6 to 6
- patch_source: int32 [8192], replicated, may hold values from -1 to 8191, as said below
- doc_lengths: int32 [32], replicated, may hold values from 1 to 4608, as said below
- out_weight: bfloat16 [8192, 4096], P('head'), may hold values from -0.5 to 0.5
Outputs:
- attn_out: bfloat16 [8192, 4096], P(('ctx', 'head'))
Inputs may be any that keep to these rules, and one draw needn't show every extreme that they name: `patch_source`: exactly one aligned block of 128 positions of each index of ctx is replaced; its rows come from 16 different indices of ctx, 8 consecutive rows from each; no counterfactual position is used twice. `doc_lengths`: the lengths sum to 8192, and one document has exactly 4608 positions.
All inputs are finite; a program needn't handle non-finite values.
Results may differ from a plain program's by a relative error of at most 0.014.
Values may be sent and summed in bfloat16 or wider, within the bound.
A program may use at most 192 MiB of HBM per device.

v0:
```python
import math

import jax
import jax.numpy as jnp
from jax import lax
from jax.sharding import PartitionSpec as P

HD = 128
BLK = 128


def attend_block(running, pieces, grouped, query_pos, query_doc, doc_ends):
    row_max, row_sum, weighted = running
    key_piece, value_piece = pieces
    piece_rows = key_piece.shape[0]
    kv_heads = grouped.shape[1]
    key_heads = key_piece.reshape(piece_rows, kv_heads, HD)
    value_heads = value_piece.reshape(piece_rows, kv_heads, HD)
    scores = jnp.einsum(
        "qhgd,khd->hgqk", grouped, key_heads, preferred_element_type=jnp.float32
    ) * (1.0 / math.sqrt(HD))
    key_pos = jnp.arange(piece_rows, dtype=jnp.int32)
    key_doc = jnp.sum((key_pos[:, None] >= doc_ends[None, :]).astype(jnp.int32), axis=1)
    visible = (
        (query_pos[:, None] >= key_pos[None, :])
        & (query_doc[:, None] == key_doc[None, :])
        & (key_pos[None, :] >= 0)
    )
    scores = jnp.where(visible, scores, -jnp.inf)
    new_max = jnp.max(scores, axis=-1)
    safe_max = jnp.where(new_max == -jnp.inf, 0.0, new_max)
    rescale = jnp.exp(row_max - safe_max)
    weights = jnp.exp(scores - safe_max[..., None])
    row_sum = row_sum * rescale + jnp.sum(weights, axis=-1)
    weighted = weighted * rescale[..., None] + jnp.einsum(
        "hgqk,khd->hgqd",
        weights.astype(jnp.bfloat16),
        value_heads,
        preferred_element_type=jnp.float32,
    )
    return (new_max, row_sum, weighted)


def per_device(
    queries, keys, values, cf_queries, cf_keys, cf_values, patch_source, doc_lengths, out_weight
):
    ctx_size = lax.axis_size("ctx")
    my_index = lax.axis_index("ctx")
    local_rows = queries.shape[0]
    group_count = min(ctx_size, 16)
    slot_cap = BLK // group_count
    source_grid = patch_source.reshape(ctx_size, local_rows)
    owner_dev = jnp.where(source_grid >= 0, source_grid // local_rows, -1)
    from_me = (owner_dev == my_index).astype(jnp.int32)
    slot_rank = jnp.cumsum(from_me, axis=1) - 1
    slot_index = jnp.arange(ctx_size, dtype=jnp.int32)[:, None] * slot_cap + slot_rank
    slot_index = jnp.where(from_me > 0, slot_index, ctx_size * slot_cap)
    local_source = jnp.clip(source_grid - my_index * local_rows, 0, local_rows - 1)
    send_table = (
        jnp.zeros((ctx_size * slot_cap,), jnp.int32)
        .at[slot_index.reshape(-1)]
        .set(local_source.reshape(-1), mode="drop")
    )
    send_queries = cf_queries[send_table].reshape(ctx_size, slot_cap, cf_queries.shape[1])
    send_keys = cf_keys[send_table].reshape(ctx_size, slot_cap, cf_keys.shape[1])
    send_values = cf_values[send_table].reshape(ctx_size, slot_cap, cf_values.shape[1])
    recv_queries, recv_keys, recv_values = (
        lax.all_to_all(send_queries, "ctx", split_axis=0, concat_axis=0, tiled=True),
        lax.all_to_all(send_keys, "ctx", split_axis=0, concat_axis=0, tiled=True),
        lax.all_to_all(send_values, "ctx", split_axis=0, concat_axis=0, tiled=True),
    )
    own_source = lax.dynamic_slice_in_dim(patch_source, my_index * local_rows, local_rows)
    patched = own_source >= 0
    source_dev = jnp.where(patched, own_source // local_rows, -1)
    source_hit = (source_dev[:, None] == jnp.arange(ctx_size, dtype=jnp.int32)[None, :]).astype(
        jnp.int32
    )
    earlier = jnp.cumsum(source_hit, axis=0) - source_hit
    recv_rank = jnp.sum(earlier * source_hit, axis=1)
    pick_slot = jnp.clip(source_dev * slot_cap + recv_rank, 0, ctx_size * slot_cap - 1)
    query_rows = jnp.where(
        patched[:, None], recv_queries.reshape(ctx_size * slot_cap, -1)[pick_slot], queries
    )
    key_rows = jnp.where(
        patched[:, None], recv_keys.reshape(ctx_size * slot_cap, -1)[pick_slot], keys
    )
    value_rows = jnp.where(
        patched[:, None], recv_values.reshape(ctx_size * slot_cap, -1)[pick_slot], values
    )
    kv_heads = keys.shape[1] // HD
    query_heads = queries.shape[1] // HD
    group_size = query_heads // kv_heads
    grouped = query_rows.reshape(local_rows, kv_heads, group_size, HD)
    doc_ends = jnp.cumsum(doc_lengths)
    query_pos = my_index * local_rows + jnp.arange(local_rows, dtype=jnp.int32)
    query_doc = jnp.sum((query_pos[:, None] >= doc_ends[None, :]).astype(jnp.int32), axis=1)
    initial = (
        jnp.full((kv_heads, group_size, local_rows), -jnp.inf, jnp.float32),
        jnp.zeros((kv_heads, group_size, local_rows), jnp.float32),
        jnp.zeros((kv_heads, group_size, local_rows, HD), jnp.float32),
    )
    pieces = (
        lax.all_gather(key_rows, "ctx", axis=0, tiled=True),
        lax.all_gather(value_rows, "ctx", axis=0, tiled=True),
    )
    first_row = jnp.int32(0)
    piece_rows = pieces[0].shape[0]
    last_doc = jnp.sum((first_row + piece_rows - 1 >= doc_ends).astype(jnp.int32))
    reaches = (first_row <= query_pos[local_rows - 1]) & (last_doc >= query_doc[0])

    def compute_block(previous):
        return attend_block(previous, pieces, grouped, query_pos, query_doc, doc_ends)

    def keep_block(previous):
        return previous

    running = lax.cond(reaches, compute_block, keep_block, initial)
    row_max, row_sum, weighted = running
    normalized = weighted / row_sum[..., None]
    attended = (
        jnp.transpose(normalized, (2, 0, 1, 3))
        .reshape(local_rows, query_heads * HD)
        .astype(jnp.bfloat16)
    )
    return lax.psum_scatter(
        jnp.dot(attended, out_weight, preferred_element_type=jnp.float32).astype(jnp.bfloat16),
        "head",
        scatter_dimension=0,
        tiled=True,
    )


def solution(mesh):
    in_specs = (
        P("ctx", "head"),
        P("ctx", "head"),
        P("ctx", "head"),
        P("ctx", "head"),
        P("ctx", "head"),
        P("ctx", "head"),
        P(),
        P(),
        P("head", None),
    )
    out_specs = P(("ctx", "head"), None)
    return jax.shard_map(
        per_device, mesh=mesh, in_specs=in_specs, out_specs=out_specs, check_vma=False
    )
```

profile of v0, /device:TPU:46, one launch (start us, length us, event | category | flops | bytes accessed | tf_op | source)
XLA Modules:
  0.0 305.8 jit_solution(17223273761956999939)
XLA Ops:
  6.5 0.0 copy-start
  6.5 0.1 broadcast_bitcast_fusion
  6.6 0.8 fusion.41
  7.5 0.6 reduce-window.24
  8.1 0.2 slice_reduce_fusion.1
  8.3 0.1 add_add_fusion
  8.4 0.8 subtract_clamp_fusion
  9.2 30.4 %scatter_custom_fusion = s32[256]{0:T(256)S(1)} fusion(s32[8192]{0:T(1024)S(1)} %get-tuple-element.51, s32[8192]{0:T(1024)S(1)} %get-tuple-element.50, s32[]{:T(128)} %constant.69.clone.1), kind=kCustom, calls=%fused_computation.90 | custom fusion | bytes 1028 | tf_op jit(solution)/shard_map/scatter | solution.py:62
  39.7 2.2 gather_fusion.4
  41.9 7.5 %all-to-all-start.2 = ((bf16[32,8,128]{2,1,0:T(8,128)(2,1)}), bf16[32,8,128]{2,1,0:T(8,128)(2,1)S(1)}, u32[]{:S(2)}, u32[]{:S(2)}) async-start(bf16[32,8,128]{2,1,0:T(8,128)(2,1)} %bitcast.22), calls=%async_computation.2 | async-start | bytes 131072 | tf_op jit(solution)/shard_map/all_to_all | solution.py:70
  49.4 0.8 fusion.42
  50.2 0.6 reduce-window.31
  50.8 0.2 slice_reduce_fusion
  51.0 0.1 fusion.37
  51.1 2.2 gather_fusion.2
  53.3 0.8 all-to-all-done.2
  54.1 6.7 %all-to-all-start.1 = ((bf16[32,8,128]{2,1,0:T(8,128)(2,1)}), bf16[32,8,128]{2,1,0:T(8,128)(2,1)S(1)}, u32[]{:S(2)}, u32[]{:S(2)}) async-start(bf16[32,8,128]{2,1,0:T(8,128)(2,1)} %bitcast.20), calls=%async_computation.1 | async-start | bytes 131072 | tf_op jit(solution)/shard_map/all_to_all | solution.py:69
  60.8 0.0 all-gather.5.cloned.1.call-start
  60.8 0.9 gather_fusion.5
  61.7 3.8 %all-to-all-done.1 = bf16[32,8,128]{2,1,0:T(8,128)(2,1)S(1)} async-done(((bf16[32,8,128]{2,1,0:T(8,128)(2,1)}), bf16[32,8,128]{2,1,0:T(8,128)(2,1)S(1)}, u32[]{:S(2)}, u32[]{:S(2)}) %all-to-all-start.1) | async-done | bytes 65568 | tf_op jit(solution)/shard_map/all_to_all | solution.py:69
  65.5 0.9 gather_fusion.3
  66.3 1.6 broadcast_select_fusion
  67.9 0.0 all-gather.5.cloned.1.call-update
  67.9 0.0 all-gather.3.cloned.1.call-start
  68.0 0.7 all-gather.3.cloned.1.call-update
  68.7 0.0 copy-done
  68.7 2.0 gather_fusion.1
  70.7 6.7 %all-to-all-start = ((bf16[32,8,1024]{2,1,0:T(8,128)(2,1)}), bf16[32,8,1024]{2,1,0:T(8,128)(2,1)S(1)}, u32[]{:S(2)}, u32[]{:S(2)}) async-start(bf16[32,8,1024]{2,1,0:T(8,128)(2,1)} %bitcast.16), calls=%async_computation | async-start | bytes 1048576 | tf_op jit(solution)/shard_map/all_to_all | solution.py:68
  77.4 0.0 reduce-scatter.2.cloned.1.call-start
  77.5 0.6 slice.18
  78.1 0.7 copy.24
  78.9 0.1 reduce-window.21
  78.9 0.1 reduce.2
  79.0 0.1 convert_reduce_fusion.1
  79.1 0.6 slice.19
  80.4 0.7 fusion.43
  82.5 3.4 %all-to-all-done = bf16[32,8,1024]{2,1,0:T(8,128)(2,1)S(1)} async-done(((bf16[32,8,1024]{2,1,0:T(8,128)(2,1)}), bf16[32,8,1024]{2,1,0:T(8,128)(2,1)S(1)}, u32[]{:S(2)}, u32[]{:S(2)}) %all-to-all-start) | async-done | bytes 524320 | tf_op jit(solution)/shard_map/all_to_all | solution.py:68
  85.8 31.4 %all-gather.5.cloned.1.call-done = bf16[8192,128]{1,0:T(8,128)(2,1)} async-done(((bf16[256,128]{1,0:T(8,128)(2,1)}), bf16[8192,128]{1,0:T(8,128)(2,1)}) %all-gather.5.cloned.1.call-update) | async-done | bytes 2097168 | tf_op jit(solution)/shard_map/all_gather | solution.py:104
  117.2 50.6 %all-gather.3.cloned.1.call-done = bf16[8192,128]{1,0:T(8,128)(2,1)} async-done(((bf16[256,128]{1,0:T(8,128)(2,1)}), bf16[8192,128]{1,0:T(8,128)(2,1)}) %all-gather.3.cloned.1.call-update) | async-done | bytes 2097168 | tf_op jit(solution)/shard_map/all_gather | solution.py:103
  167.8 79.6 %conditional.1 = (f32[1,8,256]{2,1,0:T(8,128)S(1)}, f32[1,8,256,128]{2,3,1,0:T(8,128)}) conditional(s32[]{:T(128)} %convert_element_type.43, () %tuple.13, (s32[256]{0:T(256)S(1)}, s32[256]{0:T(256)S(1)}, s32[32]{0:T(128)S(1)}, pred[256]{0:T(512)(128)(4,1)S(1)}, bf16[32,8,1024]{2,1,0:T(8,128)(2,1)S(1)}, /*index=5*/s32[256,1]{0,1:T(1,128)S(1)}, ...), branch_computations={%region_9.10_spmd, %region_10.14_spmd} | conditional | flops 8782093312 | bytes 219316624 | solution.py:117
  167.8 1.2 gather_fusion
  169.0 0.2 convert_reduce_fusion
  169.2 1.9 fusion.7
  171.1 25.8 %fusion.2 = (f32[8,256]{1,0:T(8,128)S(1)}, f32[256,8,8192]{2,0,1:T(8,128)}) fusion(pred[256,8192]{1,0:T(8,128)(4,1)S(1)} %fusion.7, bf16[8192,128]{1,0:T(8,128)(2,1)} %get-tuple-element.35, bf16[256,1024]{1,0:T(8,128)(2,1)S(1)} %gather_fusion, bf16[256,1024]{1,0:T(8,128)(2,1)} %get-tuple-element.42, pred[256]{0:T(512)(128)(4,1)S(1)} %get-tuple-element.31), kind=kOutput, calls=%fused_computation.11 | convolution fusion | flops 4345559040 | bytes 72360192 | tf_op jit(solution)/shard_map/cond/branch_1_fun/qhgd,khd->hgqk/dot_general | solution.py:19
  196.9 26.2 %fusion.16 = f32[1,8,256,128]{3,2,1,0:T(8,128)} fusion(bf16[8192,128]{1,0:T(8,128)(2,1)} %get-tuple-element.36, f32[256,8,8192]{2,0,1:T(8,128)} %get-tuple-element.49, f32[8,256]{1,0:T(8,128)S(1)} %get-tuple-element.47, pred[256,8192]{1,0:T(8,128)(4,1)S(1)} %fusion.7, f32[8,256]{1,0:T(8,128)S(1)} %get-tuple-element.46), kind=kOutput, calls=%fused_computation.21 | convolution fusion | flops 4362338304 | bytes 72368128 | tf_op jit(solution)/shard_map/cond/branch_1_fun/hgqk,khd->hgqd/dot_general | solution.py:35
  223.1 21.8 %fusion.1 = f32[8,256]{1,0:T(8,128)S(1)} fusion(f32[256,8,8192]{2,0,1:T(8,128)} %get-tuple-element.49, f32[8,256]{1,0:T(8,128)S(1)} %get-tuple-element.47, pred[256,8192]{1,0:T(8,128)(4,1)S(1)} %fusion.7), kind=kLoop, calls=%fused_computation.10 | loop fusion | flops 67106816 | bytes 69222400 | tf_op jit(solution)/shard_map/cond/branch_1_fun/reduce_sum | solution.py:34
  244.9 2.6 copy.34
  247.4 1.3 divide_convert_fusion
  248.7 7.1 %convolution_convert_fusion = bf16[256,4096]{1,0:T(8,128)(2,1)} fusion(bf16[256,1024]{0,1:T(8,128)(2,1)S(1)} %bitcast.99, bf16[1024,4096]{1,0:T(8,128)(2,1)} %param.19), kind=kOutput, calls=%fused_computation.37 | convolution fusion | flops 2148532224 | bytes 11010048 | tf_op jit(solution)/shard_map/dot_general | solution.py:126
  255.9 0.0 reduce-scatter.2.cloned.1.call-update
  255.9 43.4 %reduce-scatter.2.cloned.1.call-done = bf16[32,4096]{1,0:T(8,128)(2,1)} async-done(((bf16[256,4096]{1,0:T(8,128)(2,1)}), bf16[32,4096]{1,0:T(8,128)(2,1)}) %reduce-scatter.2.cloned.1.call-update) | async-done | bytes 262160 | tf_op jit(solution)/shard_map/reduce_scatter | solution.py:125
  (16 shorter events, 0.2 us)
Async XLA Ops:
  6.5 62.2 %copy-start = (bf16[256,1024]{1,0:T(8,128)(2,1)S(1)}, bf16[256,1024]{1,0:T(8,128)(2,1)}, u32[]{:S(2)}) copy-start(bf16[256,1024]{1,0:T(8,128)(2,1)} %param.14) | copy-start | bytes 1572868
  41.9 12.2 %all-to-all-start.2 = ((bf16[32,8,128]{2,1,0:T(8,128)(2,1)}), bf16[32,8,128]{2,1,0:T(8,128)(2,1)S(1)}, u32[]{:S(2)}, u32[]{:S(2)}) async-start(bf16[32,8,128]{2,1,0:T(8,128)(2,1)} %bitcast.22), calls=%async_computation.2 | async-start | bytes 131072 | tf_op jit(solution)/shard_map/all_to_all | solution.py:70
  54.1 11.4 %all-to-all-start.1 = ((bf16[32,8,128]{2,1,0:T(8,128)(2,1)}), bf16[32,8,128]{2,1,0:T(8,128)(2,1)S(1)}, u32[]{:S(2)}, u32[]{:S(2)}) async-start(bf16[32,8,128]{2,1,0:T(8,128)(2,1)} %bitcast.20), calls=%async_computation.1 | async-start | bytes 131072 | tf_op jit(solution)/shard_map/all_to_all | solution.py:69
  60.8 56.5 %all-gather.5.cloned.1.call-start = ((), (), s32[]{:S(2)}) async-start(), calls=%async_computation.5 | async-start | bytes 2162688 | tf_op jit(solution)/shard_map/all_gather | solution.py:104
  67.9 99.8 %all-gather.3.cloned.1.call-start = ((), (), s32[]{:S(2)}) async-start(), calls=%async_computation.4 | async-start | bytes 2162688 | tf_op jit(solution)/shard_map/all_gather | solution.py:103
  70.7 15.1 %all-to-all-start = ((bf16[32,8,1024]{2,1,0:T(8,128)(2,1)}), bf16[32,8,1024]{2,1,0:T(8,128)(2,1)S(1)}, u32[]{:S(2)}, u32[]{:S(2)}) async-start(bf16[32,8,1024]{2,1,0:T(8,128)(2,1)} %bitcast.16), calls=%async_computation | async-start | bytes 1048576 | tf_op jit(solution)/shard_map/all_to_all | solution.py:68
  77.4 221.9 %reduce-scatter.2.cloned.1.call-start = ((), (), s32[]{:S(2)}) async-start(), calls=%async_computation.6 | async-start | bytes 2359296 | tf_op jit(solution)/shard_map/reduce_scatter | solution.py:125
Sparse Core Ops, SparseCore 0:
  68.1 49.1 all-gather.4
  119.8 47.9 all-gather.2
  256.0 43.2 reduce-scatter.1
where the time goes:
time: 308 us; the launch traced here: 306 us
  waiting for transfers between devices  134 us (44%)
  matrix products  59.1 us (19%)
  local copies, waits for them, and re-layouts  44.7 us (15%)
  other arithmetic  31.7 us (10%)
  starting transfers between devices  21 us (7%)
  between operations  15.3 us (5%)
    all_gather x1, waiting for transfers between devices, per_device(): lax.all_gather(key_rows, 'ctx', axis=0, tiled=True)  50.6 us
    reduce_scatter x1, waiting for transfers between devices, per_device(): lax.psum_scatter(jnp.dot(attended, out_weight, preferred_element_type=jnp...  43.4 us
    all_gather x1, waiting for transfers between devices, per_device(): lax.all_gather(value_rows, 'ctx', axis=0, tiled=True)  31.4 us
    scatter x1, local copies, waits for them, and re-layouts, per_device(): send_table = jnp.zeros((ctx_size * slot_cap,), jnp.int32).at[slot_index.r...  30.4 us
    dot_general x1, matrix products, attend_block(): jnp.einsum('hgqk,khd->hgqd', weights.astype(jnp.bfloat16), value_heads, p...  26.2 us
    dot_general x1, matrix products, attend_block(): jnp.einsum('qhgd,khd->hgqk', grouped, key_heads, preferred_element_type=j...  25.8 us
    reduce_sum x1, other arithmetic, attend_block(): row_sum = row_sum * rescale + jnp.sum(weights, axis=-1)  21.8 us
    all_to_all x1, starting transfers between devices, per_device(): lax.all_to_all(send_values, 'ctx', split_axis=0, concat_axis=0, tiled=True)  7.51 us
  transfers between devices with their start and end apart: 6, of which 6 were waited for; matrix products, arithmetic and copies ran while one was open for 3% of the time, Pallas kernels for 0%

commit v1 on v0

v1 whole, which is shorter than its diff:
```python
import math

import jax
import jax.numpy as jnp
from jax import lax
from jax.experimental import pallas as pl
from jax.experimental.pallas import tpu as pltpu
from jax.sharding import PartitionSpec as P

HD = 128
ROWS = 256
SLOT = 8
NEAR = 9
FAR = -(2.0**19)
EXP2 = math.log2(math.e) / math.sqrt(HD)
TILES = 8
MESH = pl.DeviceIdType.MESH
F32, BF16 = jnp.float32, jnp.bfloat16
VMEM = pl.BlockSpec(memory_space=pltpu.VMEM)
ANY = pl.BlockSpec(memory_space=pl.ANY)


def iota(shape, dim):
    return lax.broadcasted_iota(jnp.int32, shape, dim)


def dot(a, b):
    return jnp.dot(a, b, preferred_element_type=F32)


def patch_kernel(
    patch_ref, q_ref, k_ref, v_ref, cq_ref, ck_ref, cv_ref,
    oq_ref, okv_ref,
    send, recv, send_sem, recv_sem,
):
    n = patch_ref.shape[0]
    heads = cq_ref.shape[1] // HD
    wide = cq_ref.shape[1]
    me = lax.axis_index("ctx")
    barrier = pltpu.get_barrier_semaphore()

    def greet(i, carry):
        pl.semaphore_signal(
            barrier, inc=1, device_id={"ctx": lax.rem(me + i, n)}, device_id_type=MESH
        )
        return carry

    lax.fori_loop(1, n, greet, 0)

    table = patch_ref[...]
    mine = (table >> 8) == me
    ones = mine.astype(F32).astype(BF16)
    upto = (iota((ROWS, ROWS), 0) <= iota((ROWS, ROWS), 1)).astype(F32).astype(BF16)
    rank = jnp.where(mine, dot(ones, upto), 0.0).astype(BF16)
    row = jnp.where(mine, (table & (ROWS - 1)).astype(F32), 0.0).astype(BF16)
    spread = ((iota((n * SLOT, n), 0) >> 3) == iota((n * SLOT, n), 1)).astype(F32).astype(BF16)
    rank_all = dot(spread, rank)
    row_all = dot(spread, row)
    slot = ((iota((n * SLOT, ROWS), 0) & (SLOT - 1)) + 1).astype(F32)
    picked = jnp.sum(
        jnp.where(rank_all == slot, row_all + 1.0, 0.0), axis=1, keepdims=True
    ) - 1.0
    lane = iota((n * SLOT, ROWS), 1).astype(F32)
    choose = (lane == picked).astype(F32).astype(BF16)
    send[:, :, wide : wide + HD] = dot(choose, ck_ref[...]).reshape(n, SLOT, HD).astype(BF16)
    send[:, :, wide + HD :] = dot(choose, cv_ref[...]).reshape(n, SLOT, HD).astype(BF16)
    send[:, :, :wide] = dot(choose, cq_ref[...]).reshape(n, SLOT, wide).astype(BF16)
    pl.semaphore_wait(barrier, n - 1)

    def copy_to(i):
        peer = lax.rem(me + i, n)
        return pltpu.make_async_remote_copy(
            src_ref=send.at[peer],
            dst_ref=recv.at[me],
            send_sem=send_sem.at[i],
            recv_sem=recv_sem.at[i],
            device_id={"ctx": peer},
            device_id_type=MESH,
        )

    def copy_from(i):
        peer = lax.rem(me + n - i, n)
        return pltpu.make_async_remote_copy(
            src_ref=send.at[peer],
            dst_ref=recv.at[peer],
            send_sem=send_sem.at[i],
            recv_sem=recv_sem.at[i],
            device_id={"ctx": peer},
            device_id_type=MESH,
        )

    def start(i, carry):
        copy_to(i).start()
        return carry

    lax.fori_loop(1, n, start, 0)
    recv[me] = send[me]

    own = (patch_ref[pl.ds(me, 1), :] >> 8).astype(F32)
    same = iota((ROWS, ROWS), 0) == iota((ROWS, ROWS), 1)
    own_col = jnp.sum(jnp.where(same, own, 0.0), axis=1, keepdims=True)
    before = (own_col == own) & (iota((ROWS, ROWS), 1) < iota((ROWS, ROWS), 0))
    place = own_col * SLOT + jnp.sum(jnp.where(before, 1.0, 0.0), axis=1, keepdims=True)
    replaced = own_col >= 0.0
    lane = iota((ROWS, n * SLOT), 1).astype(F32)
    choose = ((lane == place) & replaced).astype(F32).astype(BF16)

    def arrive(i, carry):
        copy_from(i).wait_recv()
        return carry

    lax.fori_loop(1, n, arrive, 0)

    def merge(lo, base):
        got = recv[:, :, lo : lo + HD].astype(F32).reshape(n * SLOT, HD).astype(BF16)
        return jnp.where(replaced, dot(choose, got), base.astype(F32)).astype(BF16)

    okv_ref[0] = merge(wide, k_ref[...])
    okv_ref[1] = merge(wide + HD, v_ref[...])
    for h in range(heads):
        oq_ref[h] = merge(h * HD, q_ref[:, h * HD : (h + 1) * HD])

    def sent(i, carry):
        copy_to(i).wait_send()
        return carry

    lax.fori_loop(1, n, sent, 0)


def attend_kernel(
    lens_ref, q_ref, kv_ref,
    out_ref,
    kv, top, total, acc, send_sem, recv_sem, pass_sem, got_sem,
):
    heads = q_ref.shape[0]
    n = lax.axis_size("ctx")
    me = lax.axis_index("ctx")
    chip, core = me // 2, lax.rem(me, 2)
    other = 1 - core
    back = jnp.minimum(chip, NEAR)
    ahead = jnp.minimum(n // 2 - 1 - chip, NEAR)
    partner = {"ctx": chip * 2 + other}
    barrier = pltpu.get_barrier_semaphore()

    def greet(peer):
        pl.semaphore_signal(barrier, inc=1, device_id={"ctx": peer}, device_id_type=MESH)

    greet(chip * 2 + other)

    def greet_ahead(d, carry):
        greet(me + 2 * d)
        return carry

    def greet_back(d, carry):
        greet(me - 2 * d)
        return carry

    lax.fori_loop(1, ahead + 1, greet_ahead, 0)
    lax.fori_loop(1, back + 1, greet_back, 0)

    kv[0, core] = kv_ref[...]

    @pl.when(core == 0)
    def _():
        kv[0, 1] = jnp.zeros_like(kv_ref[...])

    lens = lens_ref[...].astype(F32)
    docs = lens.shape[1]
    d0, d1 = iota((docs, HD), 0), iota((docs, HD), 1)
    eye = iota((docs, docs), 0) == iota((docs, docs), 1)
    lens_col = jnp.sum(jnp.where(eye, lens, 0.0), axis=1, keepdims=True)
    ends = jnp.sum(jnp.where(d0 <= d1, lens_col, 0.0), axis=0, keepdims=True)
    starts = jnp.sum(jnp.where(d0 < d1, lens_col, 0.0), axis=0, keepdims=True)

    def in_doc(first, rows):
        pos = (first + iota((rows, HD), 0)).astype(F32)
        return (pos >= starts) & (pos < ends)

    far = jnp.where(in_doc(me * ROWS, ROWS), 0.0, FAR).astype(BF16)
    top[...] = jnp.full_like(top, -(2.0**22))
    total[...] = jnp.zeros_like(total)
    acc[...] = jnp.zeros_like(acc)

    pl.semaphore_wait(barrier, back + ahead + 1)

    def to_chip(d):
        return pltpu.make_async_remote_copy(
            src_ref=kv_ref,
            dst_ref=kv.at[d, core],
            send_sem=send_sem.at[d],
            recv_sem=recv_sem.at[d],
            device_id={"ctx": me + 2 * d},
            device_id_type=MESH,
        )

    def from_chip(d):
        return pltpu.make_async_remote_copy(
            src_ref=kv_ref,
            dst_ref=kv.at[d, core],
            send_sem=send_sem.at[d],
            recv_sem=recv_sem.at[d],
            device_id={"ctx": me - 2 * d},
            device_id_type=MESH,
        )

    def to_partner(d):
        return pltpu.make_async_remote_copy(
            src_ref=kv.at[d, core],
            dst_ref=kv.at[d, core],
            send_sem=pass_sem.at[d],
            recv_sem=got_sem.at[d],
            device_id=partner,
            device_id_type=MESH,
        )

    def from_partner(d):
        return pltpu.make_async_remote_copy(
            src_ref=kv.at[d, other],
            dst_ref=kv.at[d, other],
            send_sem=pass_sem.at[d],
            recv_sem=got_sem.at[d],
            device_id=partner,
            device_id_type=MESH,
        )

    own_to_partner = pltpu.make_async_remote_copy(
        src_ref=kv_ref,
        dst_ref=kv.at[0, core],
        send_sem=pass_sem.at[0],
        recv_sem=got_sem.at[0],
        device_id=partner,
        device_id_type=MESH,
    )

    @pl.when(core == 0)
    def _():
        own_to_partner.start()

    def send_out(d, carry):
        to_chip(d).start()
        return carry

    lax.fori_loop(1, ahead + 1, send_out, 0)

    def relay(d):
        from_chip(d).wait_recv()
        to_partner(d).start()

    @pl.when(back >= 1)
    def _():
        relay(1)

    @pl.when(core == 1)
    def _():
        from_partner(0).wait_recv()

    def unit(d, diagonal):
        keys = jnp.concatenate([kv[d, 0, 0], kv[d, 1, 0]], axis=0)
        vals = jnp.concatenate([kv[d, 0, 1], kv[d, 1, 1]], axis=0)
        span = 2 * ROWS
        first = (chip - d) * span
        marks = jnp.where(in_doc(first, span), 1.0, 0.0).astype(BF16)
        keys = jnp.concatenate([keys, marks], axis=1)
        vals = jnp.concatenate([vals, jnp.ones((span, HD), BF16)], axis=1)

        def head(h, carry):
            rows = jnp.concatenate([q_ref[h], far], axis=1)
            scores = lax.dot_general(
                rows, keys, (((1,), (1,)), ((), ())), preferred_element_type=F32
            )
            if diagonal:
                seen = first + iota((ROWS, span), 1) <= me * ROWS + iota((ROWS, span), 0)
                scores = jnp.where(seen, scores, 8.0 * FAR)
            old = top[h]
            new = jnp.maximum(old, jnp.max(scores, axis=1, keepdims=True))
            weights = jnp.concatenate(
                [
                    jnp.exp2((scores[:, t * HD : (t + 1) * HD] - new) * EXP2).astype(BF16)
                    for t in range(span // HD)
                ],
                axis=1,
            )
            scale = jnp.exp2((old - new) * EXP2)
            mixed = dot(weights, vals)
            top[h] = new
            acc[h] = acc[h] * scale + mixed[:, :HD]
            total[h] = total[h] * scale + mixed[:, HD:]
            return carry

        lax.fori_loop(0, heads, head, 0)

    unit(0, True)

    def step(d, carry):
        @pl.when(d < back)
        def _():
            relay(d + 1)

        from_partner(d).wait_recv()
        unit(d, False)
        return carry

    lax.fori_loop(1, back + 1, step, 0)

    for h in range(heads):
        out_ref[:, h * HD : (h + 1) * HD] = (acc[h] / total[h]).astype(BF16)

    def sent(d, carry):
        to_chip(d).wait_send()
        return carry

    def passed(d, carry):
        to_partner(d).wait_send()
        return carry

    lax.fori_loop(1, ahead + 1, sent, 0)
    lax.fori_loop(1, back + 1, passed, 0)

    @pl.when(core == 0)
    def _():
        own_to_partner.wait_send()


def project_kernel(
    a_ref, w_ref,
    out_ref,
    w, part, out_buf, in_buf, w_sem, send_sem, recv_sem,
):
    n = lax.axis_size("head")
    me = lax.axis_index("head")
    up, down = lax.rem(me + 1, n), lax.rem(me + n - 1, n)
    share = out_ref.shape[0]
    cols = out_ref.shape[1] // TILES
    barrier = pltpu.get_barrier_semaphore()
    for peer in (up, down):
        pl.semaphore_signal(barrier, inc=1, device_id={"head": peer}, device_id_type=MESH)

    def fetch(t):
        return pltpu.make_async_copy(
            w_ref.at[:, pl.ds(t * cols, cols)], w.at[t], w_sem.at[t]
        )

    for t in range(TILES):
        fetch(t).start()
    pl.semaphore_wait(barrier, 2)

    half = n // 2

    def hops(t):
        return (half, n - 1 - half) if t % 2 == 0 else (n - 1 - half, half)

    def move(t, way, s):
        slot = s if way == 0 else hops(t)[0] + s
        return pltpu.make_async_remote_copy(
            src_ref=out_buf.at[t, slot],
            dst_ref=in_buf.at[t, slot],
            send_sem=send_sem.at[t, slot],
            recv_sem=recv_sem.at[t, slot],
            device_id={"head": up if way == 0 else down},
            device_id_type=MESH,
        )

    def stage(t, s):
        if s == 0:
            fetch(t).wait()
            part[t] = dot(a_ref[...], w[t]).reshape(n, share, cols)
        total = part[t, me] if s == half else None
        for way in (0, 1):
            length = hops(t)[way]
            base = 0 if way == 0 else hops(t)[0]
            if s < length:
                left = length - s
                to = lax.rem(me + (left if way == 0 else n - left), n)
                value = part[t, to]
                if s > 0:
                    move(t, way, s - 1).wait_recv()
                    value = value + in_buf[t, base + s - 1].astype(F32)
                out_buf[t, base + s] = value.astype(BF16)
                move(t, way, s).start()
            if s == half:
                move(t, way, length - 1).wait_recv()
                total = total + in_buf[t, base + length - 1].astype(F32)
        if s == half:
            out_ref[:, t * cols : (t + 1) * cols] = total.astype(BF16)

    for r in range(TILES + half):
        for s in range(half + 1):
            if 0 <= r - s < TILES:
                stage(r - s, s)
    for t in range(TILES):
        for way in (0, 1):
            for s in range(hops(t)[way]):
                move(t, way, s).wait_send()


def per_device(
    queries, keys, values, cf_queries, cf_keys, cf_values, patch_source, doc_lengths, out_weight
):
    ctx = lax.axis_size("ctx")
    group = lax.axis_size("head")
    wide = queries.shape[1]
    heads = wide // HD
    dma = pltpu.SemaphoreType.DMA
    q, kv = pl.pallas_call(
        patch_kernel,
        name="patch",
        out_shape=(
            jax.ShapeDtypeStruct((heads, ROWS, HD), BF16),
            jax.ShapeDtypeStruct((2, ROWS, HD), BF16),
        ),
        in_specs=[VMEM] * 7,
        out_specs=(VMEM, VMEM),
        scratch_shapes=[
            pltpu.VMEM((ctx, SLOT, wide + 2 * HD), BF16),
            pltpu.VMEM((ctx, SLOT, wide + 2 * HD), BF16),
            dma((ctx,)),
            dma((ctx,)),
        ],
        compiler_params=pltpu.CompilerParams(collective_id=0, has_side_effects=True),
    )(
        patch_source.reshape(ctx, ROWS), queries, keys, values, cf_queries, cf_keys, cf_values
    )
    attended = pl.pallas_call(
        attend_kernel,
        name="attend",
        out_shape=jax.ShapeDtypeStruct((ROWS, wide), BF16),
        in_specs=[VMEM] * 3,
        out_specs=VMEM,
        scratch_shapes=[
            pltpu.VMEM((NEAR + 1, 2, 2, ROWS, HD), BF16),
            pltpu.VMEM((heads, ROWS, HD), F32),
            pltpu.VMEM((heads, ROWS, HD), F32),
            pltpu.VMEM((heads, ROWS, HD), F32),
            dma((NEAR + 1,)),
            dma((NEAR + 1,)),
            dma((NEAR + 1,)),
            dma((NEAR + 1,)),
        ],
        compiler_params=pltpu.CompilerParams(collective_id=1, has_side_effects=True),
    )(doc_lengths.reshape(1, -1), q, kv)
    feats = out_weight.shape[1]
    share, cols = ROWS // group, feats // TILES
    return pl.pallas_call(
        project_kernel,
        name="project",
        out_shape=jax.ShapeDtypeStruct((share, feats), BF16),
        in_specs=[VMEM, ANY],
        out_specs=VMEM,
        scratch_shapes=[
            pltpu.VMEM((TILES, wide, cols), BF16),
            pltpu.VMEM((TILES, group, share, cols), F32),
            pltpu.VMEM((TILES, group - 1, share, cols), BF16),
            pltpu.VMEM((TILES, group - 1, share, cols), BF16),
            dma((TILES,)),
            dma((TILES, group - 1)),
            dma((TILES, group - 1)),
        ],
        compiler_params=pltpu.CompilerParams(collective_id=2, has_side_effects=True),
    )(attended, out_weight)


def solution(mesh):
    in_specs = (
        P("ctx", "head"),
        P("ctx", "head"),
        P("ctx", "head"),
        P("ctx", "head"),
        P("ctx", "head"),
        P("ctx", "head"),
        P(),
        P(),
        P("head", None),
    )
    out_specs = P(("ctx", "head"), None)
    return jax.shard_map(
        per_device, mesh=mesh, in_specs=in_specs, out_specs=out_specs, check_vma=False
    )
```

time: 308 us -> 133 us (0.43)
  waiting for transfers between devices: 134 us -> 0 us
  Pallas kernels: 0 us -> 130 us
  matrix products: 59.1 us -> 0 us
  local copies, waits for them, and re-layouts: 44.7 us -> 3.05 us
  other arithmetic: 31.7 us -> 0 us
  starting transfers between devices: 21 us -> 0 us
  between operations: 15.3 us -> 0.03 us
    pallas_call x0 -> x3, Pallas kernels: none -> 130 us  [the longest x1 73.6 us: per_device(): pl.pallas_call(attend_kernel, name='attend', out_shape=jax.ShapeDtypeStru...]
    all_gather x2 -> x0, waiting for transfers between devices: 82 us -> none  [the longest x1 50.6 us: per_device(): lax.all_gather(key_rows, 'ctx', axis=0, tiled=True)]
    dot_general x3 -> x0, matrix products: 59.1 us -> none  [the longest x1 26.2 us: attend_block(): jnp.einsum('hgqk,khd->hgqd', weights.astype(jnp.bfloat16), value_heads, p...]
    reduce_scatter x1 -> x0, waiting for transfers between devices: 43.4 us -> none  [per_device(): lax.psum_scatter(jnp.dot(attended, out_weight, preferred_element_type=jnp...]
    scatter x1 -> x0, local copies, waits for them, and re-layouts: 30.4 us -> none  [per_device(): send_table = jnp.zeros((ctx_size * slot_cap,), jnp.int32).at[slot_index.r...]
    reduce_sum x5 -> x0, other arithmetic: 22.9 us -> none  [the longest x1 21.8 us: attend_block(): row_sum = row_sum * rescale + jnp.sum(weights, axis=-1)]
    all_to_all x3 -> x0, starting transfers between devices: 20.9 us -> none  [the longest x1 7.51 us: per_device(): lax.all_to_all(send_values, 'ctx', split_axis=0, concat_axis=0, tiled=True)]
    gather x6 -> x0, local copies, waits for them, and re-layouts: 9.21 us -> none  [the longest x1 2.19 us: per_device(): cf_values[send_table].reshape(ctx_size, slot_cap, cf_values.shape[1])]
  transfers between devices with their start and end apart: 6 -> 0, of which waited for: 6 -> 0; matrix products, arithmetic and copies ran while one was open for 3% -> 0% of each run, Pallas kernels for 0% -> 0%
where the time goes in v1:
time: 133 us
  Pallas kernels  130 us (98%)
  local copies, waits for them, and re-layouts  3.05 us (2%)
    pallas_call x1, Pallas kernels, per_device(): pl.pallas_call(attend_kernel, name='attend', out_shape=jax.ShapeDtypeStru...  73.6 us
    pallas_call x1, Pallas kernels, per_device(): pl.pallas_call(project_kernel, name='project', out_shape=jax.ShapeDtypeSt...  40.7 us
    pallas_call x1, Pallas kernels, per_device(): pl.pallas_call(patch_kernel, name='patch', out_shape=(jax.ShapeDtypeStruc...  15.4 us

profile of v1, /device:TPU:46, one launch (start us, length us, event | category | flops | bytes accessed | tf_op | source)
XLA Modules:
  0.0 132.8 jit_solution(9547850847206384822)
XLA Ops:
  0.0 1.4 %reshape.7.patch_ref = s32[32,256]{1,0:T(8,128)} reshape(s32[8192]{0:T(1024)} %param.15) | data formatting | bytes 65536 | tf_op jit(solution)/shard_map/reshape | solution.py:421
  1.4 15.4 %patch.1 = (bf16[8,256,128]{2,1,0:T(8,128)(2,1)}, bf16[2,256,128]{2,1,0:T(8,128)(2,1)}) custom-call(s32[32,256]{1,0:T(8,128)} %reshape.7.patch_ref, bf16[256,1024]{1,0:T(8,128)(2,1)} %q_ref.1, bf16[256,128]{1,0:T(8,128)(2,1)} %k_ref.1, bf16[256,128]{1,0:T(8,128)(2,1)} %v_ref.1, bf16[256,1024]{1,0:T(8,128)(2,1)} %cq_ref.1, bf16[256,128]{1,0:T(8,128)(2,1)} %ck_ref.1, ...), custom_call_target="tpu_custom_call" | custom-call | tf_op jit(solution)/shard_map/patch/pallas_call | solution.py:404
  16.8 73.6 %attend.1.a_ref = bf16[256,1024]{1,0:T(8,128)(2,1)} custom-call(s32[1,32]{1,0:T(1,128)} %bitcast.1, bf16[8,256,128]{2,1,0:T(8,128)(2,1)} %get-tuple-element.7.q_ref, bf16[2,256,128]{2,1,0:T(8,128)(2,1)} %get-tuple-element.8.kv_ref), custom_call_target="tpu_custom_call" | custom-call | tf_op jit(solution)/shard_map/attend/pallas_call | solution.py:423
  90.4 40.7 %project.1 = bf16[32,4096]{1,0:T(8,128)(2,1)} custom-call(bf16[256,1024]{1,0:T(8,128)(2,1)} %attend.1.a_ref, bf16[1024,4096]{1,0:T(8,128)(2,1)} %w_ref.1), custom_call_target="tpu_custom_call" | custom-call | tf_op jit(solution)/shard_map/project/pallas_call | solution.py:443
  131.2 1.7 %copy.11 = bf16[32,4096]{1,0:T(8,128)(2,1)} copy(bf16[32,4096]{1,0:T(8,128)(2,1)} %project.1) | data formatting | bytes 524288

commit v2 on v1

--- a/solution.py
+++ b/solution.py
@@ -130,7 +130,7 @@
 def attend_kernel(
     lens_ref, q_ref, kv_ref,
     out_ref,
-    kv, top, total, acc, send_sem, recv_sem, pass_sem, got_sem,
+    rows, kv, top, total, acc, send_sem, recv_sem, pass_sem, got_sem,
 ):
     heads = q_ref.shape[0]
     n = lax.axis_size("ctx")
@@ -158,11 +158,11 @@
     lax.fori_loop(1, ahead + 1, greet_ahead, 0)
     lax.fori_loop(1, back + 1, greet_back, 0)
 
-    kv[0, core] = kv_ref[...]
+    kv[0, core, :, :, :HD] = kv_ref[...]
 
     @pl.when(core == 0)
     def _():
-        kv[0, 1] = jnp.zeros_like(kv_ref[...])
+        kv[0, 1, :, :, :HD] = jnp.zeros_like(kv_ref[...])
 
     lens = lens_ref[...].astype(F32)
     docs = lens.shape[1]
@@ -177,16 +177,25 @@
         return (pos >= starts) & (pos < ends)
 
     far = jnp.where(in_doc(me * ROWS, ROWS), 0.0, FAR).astype(BF16)
-    top[...] = jnp.full_like(top, -(2.0**22))
-    total[...] = jnp.zeros_like(total)
-    acc[...] = jnp.zeros_like(acc)
+    for h in range(heads):
+        rows[h, :, :HD] = q_ref[h]
+        rows[h, :, HD:] = far
+
+    def mark(d, carry):
+        for c in (0, 1):
+            here = in_doc(((chip - d) * 2 + c) * ROWS, ROWS)
+            kv[d, c, 0, :, HD:] = jnp.where(here, 1.0, 0.0).astype(BF16)
+            kv[d, c, 1, :, HD:] = jnp.ones((ROWS, HD), BF16)
+        return carry
+
+    lax.fori_loop(0, back + 1, mark, 0)
 
     pl.semaphore_wait(barrier, back + ahead + 1)
 
     def to_chip(d):
         return pltpu.make_async_remote_copy(
             src_ref=kv_ref,
-            dst_ref=kv.at[d, core],
+            dst_ref=kv.at[d, core, :, :, pl.ds(0, HD)],
             send_sem=send_sem.at[d],
             recv_sem=recv_sem.at[d],
             device_id={"ctx": me + 2 * d},
@@ -196,7 +205,7 @@
     def from_chip(d):
         return pltpu.make_async_remote_copy(
             src_ref=kv_ref,
-            dst_ref=kv.at[d, core],
+            dst_ref=kv.at[d, core, :, :, pl.ds(0, HD)],
             send_sem=send_sem.at[d],
             recv_sem=recv_sem.at[d],
             device_id={"ctx": me - 2 * d},
@@ -205,8 +214,8 @@
 
     def to_partner(d):
         return pltpu.make_async_remote_copy(
-            src_ref=kv.at[d, core],
-            dst_ref=kv.at[d, core],
+            src_ref=kv.at[d, core, :, :, pl.ds(0, HD)],
+            dst_ref=kv.at[d, core, :, :, pl.ds(0, HD)],
             send_sem=pass_sem.at[d],
             recv_sem=got_sem.at[d],
             device_id=partner,
@@ -215,8 +224,8 @@
 
     def from_partner(d):
         return pltpu.make_async_remote_copy(
-            src_ref=kv.at[d, other],
-            dst_ref=kv.at[d, other],
+            src_ref=kv.at[d, other, :, :, pl.ds(0, HD)],
+            dst_ref=kv.at[d, other, :, :, pl.ds(0, HD)],
             send_sem=pass_sem.at[d],
             recv_sem=got_sem.at[d],
             device_id=partner,
@@ -225,7 +234,7 @@
 
     own_to_partner = pltpu.make_async_remote_copy(
         src_ref=kv_ref,
-        dst_ref=kv.at[0, core],
+        dst_ref=kv.at[0, core, :, :, pl.ds(0, HD)],
         send_sem=pass_sem.at[0],
         recv_sem=got_sem.at[0],
         device_id=partner,
@@ -254,25 +263,25 @@
     def _():
         from_partner(0).wait_recv()
 
-    def unit(d, diagonal):
-        keys = jnp.concatenate([kv[d, 0, 0], kv[d, 1, 0]], axis=0)
-        vals = jnp.concatenate([kv[d, 0, 1], kv[d, 1, 1]], axis=0)
-        span = 2 * ROWS
-        first = (chip - d) * span
-        marks = jnp.where(in_doc(first, span), 1.0, 0.0).astype(BF16)
-        keys = jnp.concatenate([keys, marks], axis=1)
-        vals = jnp.concatenate([vals, jnp.ones((span, HD), BF16)], axis=1)
-
-        def head(h, carry):
-            rows = jnp.concatenate([q_ref[h], far], axis=1)
+    span = 2 * ROWS
+
+    def unit(d, first):
+        keys = kv[d, :, 0].reshape(span, 2 * HD)
+        vals = kv[d, :, 1].reshape(span, 2 * HD)
+        for h in range(heads):
             scores = lax.dot_general(
-                rows, keys, (((1,), (1,)), ((), ())), preferred_element_type=F32
+                rows[h], keys, (((1,), (1,)), ((), ())), preferred_element_type=F32
             )
-            if diagonal:
-                seen = first + iota((ROWS, span), 1) <= me * ROWS + iota((ROWS, span), 0)
+            if first:
+                seen = iota((ROWS, span), 1) <= core * ROWS + iota((ROWS, span), 0)
                 scores = jnp.where(seen, scores, 8.0 * FAR)
-            old = top[h]
-            new = jnp.maximum(old, jnp.max(scores, axis=1, keepdims=True))
+            new = jnp.max(scores, axis=1, keepdims=True)
+            if first:
+                new = jnp.broadcast_to(new, (ROWS, HD))
+            else:
+                old = top[h]
+                new = jnp.maximum(old, new)
+                scale = jnp.exp2((old - new) * EXP2)
             weights = jnp.concatenate(
                 [
                     jnp.exp2((scores[:, t * HD : (t + 1) * HD] - new) * EXP2).astype(BF16)
@@ -280,14 +289,14 @@
                 ],
                 axis=1,
             )
-            scale = jnp.exp2((old - new) * EXP2)
             mixed = dot(weights, vals)
             top[h] = new
-            acc[h] = acc[h] * scale + mixed[:, :HD]
-            total[h] = total[h] * scale + mixed[:, HD:]
-            return carry
-
-        lax.fori_loop(0, heads, head, 0)
+            if first:
+                acc[h] = mixed[:, :HD]
+                total[h] = mixed[:, HD:]
+            else:
+                acc[h] = acc[h] * scale + mixed[:, :HD]
+                total[h] = total[h] * scale + mixed[:, HD:]
 
     unit(0, True)
 
@@ -427,7 +436,8 @@
         in_specs=[VMEM] * 3,
         out_specs=VMEM,
         scratch_shapes=[
-            pltpu.VMEM((NEAR + 1, 2, 2, ROWS, HD), BF16),
+            pltpu.VMEM((heads, ROWS, 2 * HD), BF16),
+            pltpu.VMEM((NEAR + 1, 2, 2, ROWS, 2 * HD), BF16),
             pltpu.VMEM((heads, ROWS, HD), F32),
             pltpu.VMEM((heads, ROWS, HD), F32),
             pltpu.VMEM((heads, ROWS, HD), F32),

time: 133 us -> 102 us (0.77); the launches traced: 133 us -> 100 us
  Pallas kernels: 130 us -> 97.3 us
    pallas_call x1, Pallas kernels: 73.6 us -> 42 us  [per_device(): pl.pallas_call(attend_kernel, name='attend', out_shape=jax.ShapeDtypeStru...]
where the time goes in v2:
time: 102 us; the launch traced here: 100 us
  Pallas kernels  97.3 us (95%)
  local copies, waits for them, and re-layouts  3.05 us (3%)
    pallas_call x1, Pallas kernels, per_device(): pl.pallas_call(attend_kernel, name='attend', out_shape=jax.ShapeDtypeStru...  42 us
    pallas_call x1, Pallas kernels, per_device(): pl.pallas_call(project_kernel, name='project', out_shape=jax.ShapeDtypeSt...  39.9 us
    pallas_call x1, Pallas kernels, per_device(): pl.pallas_call(patch_kernel, name='patch', out_shape=(jax.ShapeDtypeStruc...  15.4 us

profile of v2, /device:TPU:46, one launch (start us, length us, event | category | flops | bytes accessed | tf_op | source)
XLA Modules:
  0.0 100.4 jit_solution(12379365941548530350)
XLA Ops:
  0.0 1.4 %reshape.7.patch_ref = s32[32,256]{1,0:T(8,128)} reshape(s32[8192]{0:T(1024)} %param.15) | data formatting | bytes 65536 | tf_op jit(solution)/shard_map/reshape | solution.py:430
  1.4 15.4 %patch.1 = (bf16[8,256,128]{2,1,0:T(8,128)(2,1)}, bf16[2,256,128]{2,1,0:T(8,128)(2,1)}) custom-call(s32[32,256]{1,0:T(8,128)} %reshape.7.patch_ref, bf16[256,1024]{1,0:T(8,128)(2,1)} %q_ref.1, bf16[256,128]{1,0:T(8,128)(2,1)} %k_ref.1, bf16[256,128]{1,0:T(8,128)(2,1)} %v_ref.1, bf16[256,1024]{1,0:T(8,128)(2,1)} %cq_ref.1, bf16[256,128]{1,0:T(8,128)(2,1)} %ck_ref.1, ...), custom_call_target="tpu_custom_call" | custom-call | tf_op jit(solution)/shard_map/patch/pallas_call | solution.py:413
  16.8 42.0 %attend.1.a_ref = bf16[256,1024]{1,0:T(8,128)(2,1)} custom-call(s32[1,32]{1,0:T(1,128)} %bitcast.1, bf16[8,256,128]{2,1,0:T(8,128)(2,1)} %get-tuple-element.7.q_ref, bf16[2,256,128]{2,1,0:T(8,128)(2,1)} %get-tuple-element.8.kv_ref), custom_call_target="tpu_custom_call" | custom-call | tf_op jit(solution)/shard_map/attend/pallas_call | solution.py:432
  58.8 39.9 %project.1 = bf16[32,4096]{1,0:T(8,128)(2,1)} custom-call(bf16[256,1024]{1,0:T(8,128)(2,1)} %attend.1.a_ref, bf16[1024,4096]{1,0:T(8,128)(2,1)} %w_ref.1), custom_call_target="tpu_custom_call" | custom-call | tf_op jit(solution)/shard_map/project/pallas_call | solution.py:453
  98.7 1.7 %copy.11 = bf16[32,4096]{1,0:T(8,128)(2,1)} copy(bf16[32,4096]{1,0:T(8,128)(2,1)} %project.1) | data formatting | bytes 524288

commit v3 on v2

--- a/solution.py
+++ b/solution.py
@@ -10,10 +10,10 @@
 HD = 128
 ROWS = 256
 SLOT = 8
-NEAR = 9
+SIDE = 4
 FAR = -(2.0**19)
 EXP2 = math.log2(math.e) / math.sqrt(HD)
-TILES = 8
+TILES = 4
 MESH = pl.DeviceIdType.MESH
 F32, BF16 = jnp.float32, jnp.bfloat16
 VMEM = pl.BlockSpec(memory_space=pltpu.VMEM)
@@ -135,34 +135,40 @@
     heads = q_ref.shape[0]
     n = lax.axis_size("ctx")
     me = lax.axis_index("ctx")
-    chip, core = me // 2, lax.rem(me, 2)
+    core = lax.rem(me, 2)
+    chip = me // 2
+    x, y = chip // SIDE, lax.rem(chip, SIDE)
+    last = n // (2 * SIDE) - 1
     other = 1 - core
-    back = jnp.minimum(chip, NEAR)
-    ahead = jnp.minimum(n // 2 - 1 - chip, NEAR)
+    way = 1 - 2 * core
+
+    def device(to_x, to_y):
+        return {"ctx": (to_x * SIDE + to_y) * 2 + core}
+
+    def along(step):
+        return lax.rem(y + SIDE + step, SIDE)
+
     partner = {"ctx": chip * 2 + other}
     barrier = pltpu.get_barrier_semaphore()
 
-    def greet(peer):
-        pl.semaphore_signal(barrier, inc=1, device_id={"ctx": peer}, device_id_type=MESH)
-
-    greet(chip * 2 + other)
-
-    def greet_ahead(d, carry):
-        greet(me + 2 * d)
-        return carry
-
-    def greet_back(d, carry):
-        greet(me - 2 * d)
-        return carry
-
-    lax.fori_loop(1, ahead + 1, greet_ahead, 0)
-    lax.fori_loop(1, back + 1, greet_back, 0)
-
-    kv[0, core, :, :, :HD] = kv_ref[...]
-
-    @pl.when(core == 0)
-    def _():
-        kv[0, 1, :, :, :HD] = jnp.zeros_like(kv_ref[...])
+    def greet(to):
+        pl.semaphore_signal(barrier, inc=1, device_id=to, device_id_type=MESH)
+
+    corner_out = (x + 3 <= last) & (y == SIDE - 1)
+    corner_in = (x >= 3) & (y == 0)
+    greet(partner)
+    greet(device(x, along(1)))
+    greet(device(x, along(-1)))
+    for cond, to in (
+        (x < last, device(x + 1, y)),
+        (x >= 1, device(x - 1, y)),
+        (corner_out, device(x + 3, 0)),
+        (corner_in, device(x - 3, SIDE - 1)),
+    ):
+
+        @pl.when(cond)
+        def _(to=to):
+            greet(to)
 
     lens = lens_ref[...].astype(F32)
     docs = lens.shape[1]
@@ -172,102 +178,167 @@
     ends = jnp.sum(jnp.where(d0 <= d1, lens_col, 0.0), axis=0, keepdims=True)
     starts = jnp.sum(jnp.where(d0 < d1, lens_col, 0.0), axis=0, keepdims=True)
 
-    def in_doc(first, rows):
-        pos = (first + iota((rows, HD), 0)).astype(F32)
+    def in_doc(first):
+        pos = (first + iota((ROWS, HD), 0)).astype(F32)
         return (pos >= starts) & (pos < ends)
 
-    far = jnp.where(in_doc(me * ROWS, ROWS), 0.0, FAR).astype(BF16)
+    def as_int(cond):
+        return jnp.where(cond, 1, 0)
+
+    pl.semaphore_wait(
+        barrier, 3 + as_int(x < last) + as_int(x >= 1) + as_int(corner_out) + as_int(corner_in)
+    )
+
+    def part(slot, c):
+        return kv.at[slot, c, :, :, pl.ds(0, HD)]
+
+    def remote(kind, src, slot, to):
+        return pltpu.make_async_remote_copy(
+            src_ref=src,
+            dst_ref=part(slot, core),
+            send_sem=send_sem.at[kind],
+            recv_sem=recv_sem.at[kind],
+            device_id=to,
+            device_id_type=MESH,
+        )
+
+    def needs(dx, source, to):
+        there = x >= dx
+        near = jnp.where(dx == 0, to > source, True)
+        far = jnp.where(dx == 2, source >= to - 1, True)
+        corner = jnp.where(dx == 3, (to == 0) & (source == SIDE - 1), True)
+        return there & near & far & corner
+
+    def held(dx):
+        return kv_ref if dx == 0 else part(dx * SIDE + y, core)
+
+    def outgoing():
+        yield 0, x < last, remote(0, kv_ref, SIDE + y, device(x + 1, y))
+        yield 1, (x >= 1) & (x < last), remote(
+            1, part(SIDE + y, core), 2 * SIDE + y, device(x + 1, y)
+        )
+        yield 2, corner_out, remote(2, kv_ref, 4 * SIDE - 1, device(x + 3, 0))
+        for dx in range(3):
+            yield 3 + dx, needs(dx, y, along(way)) | needs(dx, y, along(2)), remote(
+                3 + dx, held(dx), dx * SIDE + y, device(x, along(way))
+            )
+            yield 6 + dx, needs(dx, y, along(-way)), remote(
+                6 + dx, held(dx), dx * SIDE + y, device(x, along(-way))
+            )
+            slot = dx * SIDE + along(-way)
+            yield 9 + dx, needs(dx, along(-way), along(way)), remote(
+                9 + dx, part(slot, core), slot, device(x, along(way))
+            )
+
+    sends = {kind: (cond, copy) for kind, cond, copy in outgoing()}
+
+    def arriving():
+        yield 0, x >= 1, x >= 1, SIDE + y, device(x - 1, y)
+        yield 1, x >= 2, x >= 2, 2 * SIDE + y, device(x - 1, y)
+        yield 2, corner_in, corner_in, 4 * SIDE - 1, device(x - 3, SIDE - 1)
+        for dx in range(3):
+            source = along(-way)
+            read = needs(dx, source, y)
+            yield 3 + dx, read | needs(dx, source, along(way)), read, dx * SIDE + source, device(
+                x, source
+            )
+            source = along(way)
+            read = needs(dx, source, y)
+            yield 6 + dx, read, read, dx * SIDE + source, device(x, source)
+            source = along(2)
+            read = needs(dx, source, y)
+            yield 9 + dx, read, read, dx * SIDE + source, device(x, along(-way))
+
+    arrivals = {kind: rest for kind, *rest in arriving()}
+
+    def start(*kinds):
+        for kind in kinds:
+            cond, copy = sends[kind]
+
+            @pl.when(cond)
+            def _(copy=copy):
+                copy.start()
+
+    def relay(slot):
+        return pltpu.make_async_remote_copy(
+            src_ref=part(slot, core),
+            dst_ref=part(slot, core),
+            send_sem=pass_sem.at[slot],
+            recv_sem=got_sem.at[slot],
+            device_id=partner,
+            device_id_type=MESH,
+        )
+
+    def relayed(slot):
+        return pltpu.make_async_remote_copy(
+            src_ref=part(slot, other),
+            dst_ref=part(slot, other),
+            send_sem=pass_sem.at[slot],
+            recv_sem=got_sem.at[slot],
+            device_id=partner,
+            device_id_type=MESH,
+        )
+
+    def take(kind, *then):
+        cond, read, slot, origin = arrivals[kind]
+
+        @pl.when(cond)
+        def _():
+            remote(kind, kv_ref, slot, origin).wait_recv()
+
+        start(*then)
+
+        @pl.when(read)
+        def _():
+            relay(slot).start()
+
+    own_to_partner = pltpu.make_async_remote_copy(
+        src_ref=kv_ref,
+        dst_ref=part(y, core),
+        send_sem=pass_sem.at[y],
+        recv_sem=got_sem.at[y],
+        device_id=partner,
+        device_id_type=MESH,
+    )
+    start(0, 3, 6, 2)
+
+    @pl.when(core == 0)
+    def _():
+        own_to_partner.start()
+
+    far = jnp.where(in_doc(me * ROWS), 0.0, FAR).astype(BF16)
     for h in range(heads):
         rows[h, :, :HD] = q_ref[h]
         rows[h, :, HD:] = far
-
-    def mark(d, carry):
-        for c in (0, 1):
-            here = in_doc(((chip - d) * 2 + c) * ROWS, ROWS)
-            kv[d, c, 0, :, HD:] = jnp.where(here, 1.0, 0.0).astype(BF16)
-            kv[d, c, 1, :, HD:] = jnp.ones((ROWS, HD), BF16)
-        return carry
-
-    lax.fori_loop(0, back + 1, mark, 0)
-
-    pl.semaphore_wait(barrier, back + ahead + 1)
-
-    def to_chip(d):
-        return pltpu.make_async_remote_copy(
-            src_ref=kv_ref,
-            dst_ref=kv.at[d, core, :, :, pl.ds(0, HD)],
-            send_sem=send_sem.at[d],
-            recv_sem=recv_sem.at[d],
-            device_id={"ctx": me + 2 * d},
-            device_id_type=MESH,
-        )
-
-    def from_chip(d):
-        return pltpu.make_async_remote_copy(
-            src_ref=kv_ref,
-            dst_ref=kv.at[d, core, :, :, pl.ds(0, HD)],
-            send_sem=send_sem.at[d],
-            recv_sem=recv_sem.at[d],
-            device_id={"ctx": me - 2 * d},
-            device_id_type=MESH,
-        )
-
-    def to_partner(d):
-        return pltpu.make_async_remote_copy(
-            src_ref=kv.at[d, core, :, :, pl.ds(0, HD)],
-            dst_ref=kv.at[d, core, :, :, pl.ds(0, HD)],
-            send_sem=pass_sem.at[d],
-            recv_sem=got_sem.at[d],
-            device_id=partner,
-            device_id_type=MESH,
-        )
-
-    def from_partner(d):
-        return pltpu.make_async_remote_copy(
-            src_ref=kv.at[d, other, :, :, pl.ds(0, HD)],
-            dst_ref=kv.at[d, other, :, :, pl.ds(0, HD)],
-            send_sem=pass_sem.at[d],
-            recv_sem=got_sem.at[d],
-            device_id=partner,
-            device_id_type=MESH,
-        )
-
-    own_to_partner = pltpu.make_async_remote_copy(
-        src_ref=kv_ref,
-        dst_ref=kv.at[0, core, :, :, pl.ds(0, HD)],
-        send_sem=pass_sem.at[0],
-        recv_sem=got_sem.at[0],
-        device_id=partner,
-        device_id_type=MESH,
-    )
+    kv[y, core, :, :, :HD] = kv_ref[...]
 
     @pl.when(core == 0)
     def _():
-        own_to_partner.start()
-
-    def send_out(d, carry):
-        to_chip(d).start()
+        kv[y, 1, :, :, :HD] = jnp.zeros_like(kv_ref[...])
+
+    def mark(slot):
+        dx, source = slot // SIDE, lax.rem(slot, SIDE)
+        for c in (0, 1):
+            here = in_doc((((x - dx) * SIDE + source) * 2 + c) * ROWS)
+            kv[slot, c, 0, :, HD:] = jnp.where(here, 1.0, 0.0).astype(BF16)
+            kv[slot, c, 1, :, HD:] = jnp.ones((ROWS, HD), BF16)
+
+    def mark_one(slot, carry):
+        mark(slot)
         return carry
 
-    lax.fori_loop(1, ahead + 1, send_out, 0)
-
-    def relay(d):
-        from_chip(d).wait_recv()
-        to_partner(d).start()
-
-    @pl.when(back >= 1)
-    def _():
-        relay(1)
+    lax.fori_loop(0, 3 * SIDE, mark_one, 0)
+    mark(4 * SIDE - 1)
 
     @pl.when(core == 1)
     def _():
-        from_partner(0).wait_recv()
+        relayed(y).wait_recv()
 
     span = 2 * ROWS
 
-    def unit(d, first):
-        keys = kv[d, :, 0].reshape(span, 2 * HD)
-        vals = kv[d, :, 1].reshape(span, 2 * HD)
+    def unit(slot, first):
+        keys = kv[slot, :, 0].reshape(span, 2 * HD)
+        vals = kv[slot, :, 1].reshape(span, 2 * HD)
         for h in range(heads):
             scores = lax.dot_general(
                 rows[h], keys, (((1,), (1,)), ((), ())), preferred_element_type=F32
@@ -298,32 +369,68 @@
                 acc[h] = acc[h] * scale + mixed[:, :HD]
                 total[h] = total[h] * scale + mixed[:, HD:]
 
-    unit(0, True)
-
-    def step(d, carry):
-        @pl.when(d < back)
+    unit(y, True)
+
+    order = ((1, 0), (0, 1), (0, 3), (2, 0), (1, 1), (1, 3),
+             (0, 2), (2, 1), (2, 3), (1, 2), (3, 3), (2, 2))
+    code_x = sum(dx << (2 * i) for i, (dx, _) in enumerate(order))
+    code_y = sum(dy << (2 * i) for i, (_, dy) in enumerate(order))
+
+    def serve(i):
+        if i == 0:
+            take(0, 1, 4, 7)
+            take(3, 9)
+            take(6)
+        if i == 3:
+            take(1, 5, 8)
+        if i == 4:
+            take(4, 10)
+            take(7)
+            take(9)
+        if i == 7:
+            take(5, 11)
+            take(8)
+        if i == 9:
+            take(10)
+            take(2)
+        if i == 11:
+            take(11)
+
+    def step(i, carry):
+        for at in (0, 3, 4, 7, 9, 11):
+
+            @pl.when(i == at)
+            def _(at=at):
+                serve(at)
+
+        dx = (code_x >> (2 * i)) & 3
+        source = lax.rem(y + ((code_y >> (2 * i)) & 3), SIDE)
+        slot = dx * SIDE + source
+
+        @pl.when(needs(dx, source, y))
         def _():
-            relay(d + 1)
-
-        from_partner(d).wait_recv()
-        unit(d, False)
+            relayed(slot).wait_recv()
+            unit(slot, False)
+
         return carry
 
-    lax.fori_loop(1, back + 1, step, 0)
+    lax.fori_loop(0, len(order), step, 0)
 
     for h in range(heads):
         out_ref[:, h * HD : (h + 1) * HD] = (acc[h] / total[h]).astype(BF16)
 
-    def sent(d, carry):
-        to_chip(d).wait_send()
-        return carry
-
-    def passed(d, carry):
-        to_partner(d).wait_send()
-        return carry
-
-    lax.fori_loop(1, ahead + 1, sent, 0)
-    lax.fori_loop(1, back + 1, passed, 0)
+    for kind in range(12):
+        cond, copy = sends[kind]
+
+        @pl.when(cond)
+        def _(copy=copy):
+            copy.wait_send()
+
+        _, read, slot, _ = arrivals[kind]
+
+        @pl.when(read)
+        def _(slot=slot):
+            relay(slot).wait_send()
 
     @pl.when(core == 0)
     def _():
@@ -392,10 +499,9 @@
         if s == half:
             out_ref[:, t * cols : (t + 1) * cols] = total.astype(BF16)
 
-    for r in range(TILES + half):
-        for s in range(half + 1):
-            if 0 <= r - s < TILES:
-                stage(r - s, s)
+    for s in range(half + 1):
+        for t in range(TILES):
+            stage(t, s)
     for t in range(TILES):
         for way in (0, 1):
             for s in range(hops(t)[way]):
@@ -437,14 +543,14 @@
         out_specs=VMEM,
         scratch_shapes=[
             pltpu.VMEM((heads, ROWS, 2 * HD), BF16),
-            pltpu.VMEM((NEAR + 1, 2, 2, ROWS, 2 * HD), BF16),
+            pltpu.VMEM((4 * SIDE, 2, 2, ROWS, 2 * HD), BF16),
             pltpu.VMEM((heads, ROWS, HD), F32),
             pltpu.VMEM((heads, ROWS, HD), F32),
             pltpu.VMEM((heads, ROWS, HD), F32),
-            dma((NEAR + 1,)),
-            dma((NEAR + 1,)),
-            dma((NEAR + 1,)),
-            dma((NEAR + 1,)),
+            dma((12,)),
+            dma((12,)),
+            dma((4 * SIDE,)),
+            dma((4 * SIDE,)),
         ],
         compiler_params=pltpu.CompilerParams(collective_id=1, has_side_effects=True),
     )(doc_lengths.reshape(1, -1), q, kv)

time: 102 us -> 86.3 us (0.85)
  the two profiles are of different devices: /device:TPU:46 before, /device:TPU:7 now
where the time goes in v3:
time: 86.3 us; the launch traced here: 86.1 us
  Pallas kernels  83 us (96%)
  local copies, waits for them, and re-layouts  3.05 us (4%)
    pallas_call x1, Pallas kernels, per_device(): pl.pallas_call(attend_kernel, name='attend', out_shape=jax.ShapeDtypeStru...  35.9 us
    pallas_call x1, Pallas kernels, per_device(): pl.pallas_call(project_kernel, name='project', out_shape=jax.ShapeDtypeSt...  30.4 us
    pallas_call x1, Pallas kernels, per_device(): pl.pallas_call(patch_kernel, name='patch', out_shape=(jax.ShapeDtypeStruc...  16.7 us

profile of v3, /device:TPU:7, one launch (start us, length us, event | category | flops | bytes accessed | tf_op | source)
XLA Modules:
  0.0 86.1 jit_solution(7150618343860864568)
XLA Ops:
  0.0 1.4 %reshape.7.patch_ref = s32[32,256]{1,0:T(8,128)} reshape(s32[8192]{0:T(1024)} %param.15) | data formatting | bytes 65536 | tf_op jit(solution)/shard_map/reshape | solution.py:536
  1.4 16.7 %patch.1 = (bf16[8,256,128]{2,1,0:T(8,128)(2,1)}, bf16[2,256,128]{2,1,0:T(8,128)(2,1)}) custom-call(s32[32,256]{1,0:T(8,128)} %reshape.7.patch_ref, bf16[256,1024]{1,0:T(8,128)(2,1)} %q_ref.1, bf16[256,128]{1,0:T(8,128)(2,1)} %k_ref.1, bf16[256,128]{1,0:T(8,128)(2,1)} %v_ref.1, bf16[256,1024]{1,0:T(8,128)(2,1)} %cq_ref.1, bf16[256,128]{1,0:T(8,128)(2,1)} %ck_ref.1, ...), custom_call_target="tpu_custom_call" | custom-call | tf_op jit(solution)/shard_map/patch/pallas_call | solution.py:519
  18.1 35.9 %attend.1.a_ref = bf16[256,1024]{1,0:T(8,128)(2,1)} custom-call(s32[1,32]{1,0:T(1,128)} %bitcast.1, bf16[8,256,128]{2,1,0:T(8,128)(2,1)} %get-tuple-element.7.q_ref, bf16[2,256,128]{2,1,0:T(8,128)(2,1)} %get-tuple-element.8.kv_ref), custom_call_target="tpu_custom_call" | custom-call | tf_op jit(solution)/shard_map/attend/pallas_call | solution.py:538
  54.0 30.4 %project.1 = bf16[32,4096]{1,0:T(8,128)(2,1)} custom-call(bf16[256,1024]{1,0:T(8,128)(2,1)} %attend.1.a_ref, bf16[1024,4096]{1,0:T(8,128)(2,1)} %w_ref.1), custom_call_target="tpu_custom_call" | custom-call | tf_op jit(solution)/shard_map/project/pallas_call | solution.py:559
  84.4 1.7 %copy.11 = bf16[32,4096]{1,0:T(8,128)(2,1)} copy(bf16[32,4096]{1,0:T(8,128)(2,1)} %project.1) | data formatting | bytes 524288

commit v4 on v3

v4 whole, which is shorter than its diff:
```python
import math

import jax
import jax.numpy as jnp
from jax import lax
from jax.experimental import pallas as pl
from jax.experimental.pallas import tpu as pltpu
from jax.sharding import PartitionSpec as P

HD = 128
ROWS = 256
BLK = 128
SLOT = 8
SIDE = 4
FAR = -(2.0**19)
EXP2 = math.log2(math.e) / math.sqrt(HD)
TILES = 4
MESH = pl.DeviceIdType.MESH
F32, BF16 = jnp.float32, jnp.bfloat16
VMEM = pl.BlockSpec(memory_space=pltpu.VMEM)
ANY = pl.BlockSpec(memory_space=pl.ANY)


def iota(shape, dim):
    return lax.broadcasted_iota(jnp.int32, shape, dim)


def dot(a, b):
    return jnp.dot(a, b, preferred_element_type=F32)


def layer_kernel(
    patch_ref, lens_ref, q_ref, k_ref, v_ref, cq_ref, ck_ref, cv_ref, w_ref,
    out_ref,
    give_kv, take_kv, give_q, take_q, own, rows, kv, top, total, acc, mixed_heads,
    w, part_sum, out_buf, in_buf,
    give_kv_sem, take_kv_sem, give_q_sem, take_q_sem,
    send_sem, recv_sem, pass_sem, got_sem, w_sem, up_sem, down_sem,
):
    wide = cq_ref.shape[1]
    heads = wide // HD
    n = lax.axis_size("ctx")
    me = lax.axis_index("ctx")
    core = lax.rem(me, 2)
    chip = me // 2
    x, y = chip // SIDE, lax.rem(chip, SIDE)
    last = n // (2 * SIDE) - 1
    other = 1 - core
    way = 1 - 2 * core
    groups = lax.axis_size("head")
    group = lax.axis_index("head")
    up, down = lax.rem(group + 1, groups), lax.rem(group + groups - 1, groups)
    share = out_ref.shape[0]
    cols = out_ref.shape[1] // TILES

    barrier = pltpu.get_barrier_semaphore()

    def greet(i, carry):
        pl.semaphore_signal(
            barrier, inc=1, device_id={"ctx": lax.rem(me + i, n)}, device_id_type=MESH
        )
        return carry

    lax.fori_loop(1, n, greet, 0)
    for peer in (up, down):
        pl.semaphore_signal(barrier, inc=1, device_id={"head": peer}, device_id_type=MESH)

    def fetch(t):
        return pltpu.make_async_copy(
            w_ref.at[:, pl.ds(t * cols, cols)], w.at[t], w_sem.at[t]
        )

    for t in range(TILES):
        fetch(t).start()

    table = patch_ref[...]
    mine = (table >> 8) == me
    ones = mine.astype(F32).astype(BF16)
    upto = (iota((BLK, BLK), 0) <= iota((BLK, BLK), 1)).astype(F32).astype(BF16)
    rank = jnp.where(mine, dot(ones, upto), 0.0).astype(BF16)
    row = jnp.where(mine, (table & (ROWS - 1)).astype(F32), 0.0).astype(BF16)
    spread = (iota((n * SLOT, 2 * n), 0) >> 3) == (iota((n * SLOT, 2 * n), 1) >> 1)
    spread = spread.astype(F32).astype(BF16)
    rank_all = dot(spread, rank)
    row_all = dot(spread, row)
    slots = ((iota((n * SLOT, BLK), 0) & (SLOT - 1)) + 1).astype(F32)
    picked = jnp.sum(
        jnp.where(rank_all == slots, row_all + 1.0, 0.0), axis=1, keepdims=True
    ) - 1.0
    lane = iota((n * SLOT, ROWS), 1).astype(F32)
    choose = (lane == picked).astype(F32).astype(BF16)
    give_kv[:, :, :HD] = dot(choose, ck_ref[...]).reshape(n, SLOT, HD).astype(BF16)
    give_kv[:, :, HD:] = dot(choose, cv_ref[...]).reshape(n, SLOT, HD).astype(BF16)
    give_q[...] = dot(choose, cq_ref[...]).reshape(n, SLOT, wide).astype(BF16)

    def give(src, dst, out_sem, in_sem, i):
        peer = lax.rem(me + i, n)
        return pltpu.make_async_remote_copy(
            src_ref=src.at[peer],
            dst_ref=dst.at[me],
            send_sem=out_sem.at[i],
            recv_sem=in_sem.at[i],
            device_id={"ctx": peer},
            device_id_type=MESH,
        )

    def given(src, dst, out_sem, in_sem, i):
        peer = lax.rem(me + n - i, n)
        return pltpu.make_async_remote_copy(
            src_ref=src.at[peer],
            dst_ref=dst.at[peer],
            send_sem=out_sem.at[i],
            recv_sem=in_sem.at[i],
            device_id={"ctx": peer},
            device_id_type=MESH,
        )

    kv_rows = (give_kv, take_kv, give_kv_sem, take_kv_sem)
    q_rows = (give_q, take_q, give_q_sem, take_q_sem)

    def each(action):
        def body(i, carry):
            action(i)
            return carry

        lax.fori_loop(1, n, body, 0)

    pl.semaphore_wait(barrier, n - 1 + 2)
    each(lambda i: give(*kv_rows, i).start())
    each(lambda i: give(*q_rows, i).start())
    take_kv[me] = give_kv[me]
    take_q[me] = give_q[me]

    bound = jnp.concatenate(
        [patch_ref[pl.ds(2 * me, 1), :], patch_ref[pl.ds(2 * me + 1, 1), :]], axis=1
    )
    bound = (bound >> 8).astype(F32)
    same = iota((ROWS, ROWS), 0) == iota((ROWS, ROWS), 1)
    origin_col = jnp.sum(jnp.where(same, bound, 0.0), axis=1, keepdims=True)
    before = (origin_col == bound) & (iota((ROWS, ROWS), 1) < iota((ROWS, ROWS), 0))
    place = origin_col * SLOT + jnp.sum(jnp.where(before, 1.0, 0.0), axis=1, keepdims=True)
    replaced = origin_col >= 0.0
    lane = iota((ROWS, n * SLOT), 1).astype(F32)
    settle = ((lane == place) & replaced).astype(F32).astype(BF16)

    def merge(got, base):
        got = got.astype(F32).reshape(n * SLOT, HD).astype(BF16)
        return jnp.where(replaced, dot(settle, got), base.astype(F32)).astype(BF16)

    lens = lens_ref[...].astype(F32)
    docs = lens.shape[1]
    d0, d1 = iota((docs, HD), 0), iota((docs, HD), 1)
    eye = iota((docs, docs), 0) == iota((docs, docs), 1)
    lens_col = jnp.sum(jnp.where(eye, lens, 0.0), axis=1, keepdims=True)
    ends = jnp.sum(jnp.where(d0 <= d1, lens_col, 0.0), axis=0, keepdims=True)
    starts = jnp.sum(jnp.where(d0 < d1, lens_col, 0.0), axis=0, keepdims=True)

    def in_doc(first):
        pos = (first + iota((ROWS, HD), 0)).astype(F32)
        return (pos >= starts) & (pos < ends)

    corner_out = (x + 3 <= last) & (y == SIDE - 1)
    corner_in = (x >= 3) & (y == 0)
    partner = {"ctx": chip * 2 + other}

    def device(to_x, to_y):
        return {"ctx": (to_x * SIDE + to_y) * 2 + core}

    def along(step):
        return lax.rem(y + SIDE + step, SIDE)

    def part(slot, c):
        return kv.at[slot, c, :, :, pl.ds(0, HD)]

    def remote(kind, src, slot, to):
        return pltpu.make_async_remote_copy(
            src_ref=src,
            dst_ref=part(slot, core),
            send_sem=send_sem.at[kind],
            recv_sem=recv_sem.at[kind],
            device_id=to,
            device_id_type=MESH,
        )

    def needs(dx, source, to):
        there = x >= dx
        near = jnp.where(dx == 0, to > source, True)
        far = jnp.where(dx == 2, source >= to - 1, True)
        corner = jnp.where(dx == 3, (to == 0) & (source == SIDE - 1), True)
        return there & near & far & corner

    def held(dx):
        return own if dx == 0 else part(dx * SIDE + y, core)

    def outgoing():
        yield 0, x < last, remote(0, own, SIDE + y, device(x + 1, y))
        yield 1, (x >= 1) & (x < last), remote(
            1, part(SIDE + y, core), 2 * SIDE + y, device(x + 1, y)
        )
        yield 2, corner_out, remote(2, own, 4 * SIDE - 1, device(x + 3, 0))
        for dx in range(3):
            yield 3 + dx, needs(dx, y, along(way)) | needs(dx, y, along(2)), remote(
                3 + dx, held(dx), dx * SIDE + y, device(x, along(way))
            )
            yield 6 + dx, needs(dx, y, along(-way)), remote(
                6 + dx, held(dx), dx * SIDE + y, device(x, along(-way))
            )
            slot = dx * SIDE + along(-way)
            yield 9 + dx, needs(dx, along(-way), along(way)), remote(
                9 + dx, part(slot, core), slot, device(x, along(way))
            )

    sends = {kind: (cond, copy) for kind, cond, copy in outgoing()}

    def arriving():
        yield 0, x >= 1, x >= 1, SIDE + y, device(x - 1, y)
        yield 1, x >= 2, x >= 2, 2 * SIDE + y, device(x - 1, y)
        yield 2, corner_in, corner_in, 4 * SIDE - 1, device(x - 3, SIDE - 1)
        for dx in range(3):
            source = along(-way)
            read = needs(dx, source, y)
            yield 3 + dx, read | needs(dx, source, along(way)), read, dx * SIDE + source, device(
                x, source
            )
            source = along(way)
            read = needs(dx, source, y)
            yield 6 + dx, read, read, dx * SIDE + source, device(x, source)
            source = along(2)
            read = needs(dx, source, y)
            yield 9 + dx, read, read, dx * SIDE + source, device(x, along(-way))

    arrivals = {kind: rest for kind, *rest in arriving()}

    def start(*kinds):
        for kind in kinds:
            cond, copy = sends[kind]

            @pl.when(cond)
            def _(copy=copy):
                copy.start()

    def relay(slot):
        return pltpu.make_async_remote_copy(
            src_ref=part(slot, core),
            dst_ref=part(slot, core),
            send_sem=pass_sem.at[slot],
            recv_sem=got_sem.at[slot],
            device_id=partner,
            device_id_type=MESH,
        )

    def relayed(slot):
        return pltpu.make_async_remote_copy(
            src_ref=part(slot, other),
            dst_ref=part(slot, other),
            send_sem=pass_sem.at[slot],
            recv_sem=got_sem.at[slot],
            device_id=partner,
            device_id_type=MESH,
        )

    def take(kind, *then):
        cond, read, slot, origin = arrivals[kind]

        @pl.when(cond)
        def _():
            remote(kind, own, slot, origin).wait_recv()

        start(*then)

        @pl.when(read)
        def _():
            relay(slot).start()

    own_to_partner = pltpu.make_async_remote_copy(
        src_ref=own,
        dst_ref=part(y, core),
        send_sem=pass_sem.at[y],
        recv_sem=got_sem.at[y],
        device_id=partner,
        device_id_type=MESH,
    )
    each(lambda i: given(*kv_rows, i).wait_recv())
    fresh_k = merge(take_kv[:, :, :HD], k_ref[...])
    fresh_v = merge(take_kv[:, :, HD:], v_ref[...])
    own[0] = fresh_k
    own[1] = fresh_v
    kv[y, core, 0, :, :HD] = fresh_k
    kv[y, core, 1, :, :HD] = fresh_v

    @pl.when(core == 0)
    def _():
        kv[y, 1, :, :, :HD] = jnp.zeros_like(own[...])

    start(0, 3, 6, 2)

    @pl.when(core == 0)
    def _():
        own_to_partner.start()

    def mark(slot):
        dx, source = slot // SIDE, lax.rem(slot, SIDE)
        for c in (0, 1):
            here = in_doc((((x - dx) * SIDE + source) * 2 + c) * ROWS)
            kv[slot, c, 0, :, HD:] = jnp.where(here, 1.0, 0.0).astype(BF16)
            kv[slot, c, 1, :, HD:] = jnp.ones((ROWS, HD), BF16)

    def mark_one(slot, carry):
        mark(slot)
        return carry

    lax.fori_loop(0, 3 * SIDE, mark_one, 0)
    mark(4 * SIDE - 1)

    far = jnp.where(in_doc(me * ROWS), 0.0, FAR).astype(BF16)
    each(lambda i: given(*q_rows, i).wait_recv())
    for h in range(heads):
        lanes = slice(h * HD, (h + 1) * HD)
        rows[h, :, :HD] = merge(take_q[:, :, lanes], q_ref[:, lanes])
        rows[h, :, HD:] = far

    span = 2 * ROWS

    def unit(slot, first):
        keys = kv[slot, :, 0].reshape(span, 2 * HD)
        vals = kv[slot, :, 1].reshape(span, 2 * HD)
        for h in range(heads):
            scores = lax.dot_general(
                rows[h], keys, (((1,), (1,)), ((), ())), preferred_element_type=F32
            )
            if first:
                seen = iota((ROWS, span), 1) <= core * ROWS + iota((ROWS, span), 0)
                scores = jnp.where(seen, scores, 8.0 * FAR)
            new = jnp.max(scores, axis=1, keepdims=True)
            if first:
                new = jnp.broadcast_to(new, (ROWS, HD))
            else:
                old = top[h]
                new = jnp.maximum(old, new)
                scale = jnp.exp2((old - new) * EXP2)
            weights = jnp.concatenate(
                [
                    jnp.exp2((scores[:, t * HD : (t + 1) * HD] - new) * EXP2).astype(BF16)
                    for t in range(span // HD)
                ],
                axis=1,
            )
            mixed = dot(weights, vals)
            top[h] = new
            if first:
                acc[h] = mixed[:, :HD]
                total[h] = mixed[:, HD:]
            else:
                acc[h] = acc[h] * scale + mixed[:, :HD]
                total[h] = total[h] * scale + mixed[:, HD:]

    order = ((1, 0), (0, 1), (0, 3), (2, 0), (1, 1), (1, 3),
             (0, 2), (2, 1), (2, 3), (1, 2), (3, 3), (2, 2))
    code_x = sum(dx << (2 * i) for i, (dx, _) in enumerate(order))
    code_y = sum(dy << (2 * i) for i, (_, dy) in enumerate(order))

    def serve(i):
        if i == 0:
            take(0, 1, 4, 7)
            take(3, 9)
            take(6)
        if i == 3:
            take(1, 5, 8)
        if i == 4:
            take(4, 10)
            take(7)
            take(9)
        if i == 7:
            take(5, 11)
            take(8)
        if i == 9:
            take(10)
            take(2)
        if i == 11:
            take(11)

    serve(0)

    @pl.when(core == 1)
    def _():
        relayed(y).wait_recv()

    unit(y, True)

    def step(i, carry):
        for at in (3, 4, 7, 9, 11):

            @pl.when(i == at)
            def _(at=at):
                serve(at)

        dx = (code_x >> (2 * i)) & 3
        source = lax.rem(y + ((code_y >> (2 * i)) & 3), SIDE)
        slot = dx * SIDE + source

        @pl.when(needs(dx, source, y))
        def _():
            relayed(slot).wait_recv()
            unit(slot, False)

        return carry

    lax.fori_loop(0, len(order), step, 0)

    for h in range(heads):
        mixed_heads[:, h * HD : (h + 1) * HD] = (acc[h] / total[h]).astype(BF16)

    half = groups // 2

    def hops(t):
        return (half, groups - 1 - half) if t % 2 == 0 else (groups - 1 - half, half)

    def move(t, way, s):
        slot = s if way == 0 else hops(t)[0] + s
        return pltpu.make_async_remote_copy(
            src_ref=out_buf.at[t, slot],
            dst_ref=in_buf.at[t, slot],
            send_sem=up_sem.at[t, slot],
            recv_sem=down_sem.at[t, slot],
            device_id={"head": up if way == 0 else down},
            device_id_type=MESH,
        )

    def stage(t, s):
        if s == 0:
            fetch(t).wait()
            part_sum[t] = dot(mixed_heads[...], w[t]).reshape(groups, share, cols)
        result = part_sum[t, group] if s == half else None
        for way in (0, 1):
            length = hops(t)[way]
            base = 0 if way == 0 else hops(t)[0]
            if s < length:
                left = length - s
                to = lax.rem(group + (left if way == 0 else groups - left), groups)
                value = part_sum[t, to]
                if s > 0:
                    move(t, way, s - 1).wait_recv()
                    value = value + in_buf[t, base + s - 1].astype(F32)
                out_buf[t, base + s] = value.astype(BF16)
                move(t, way, s).start()
            if s == half:
                move(t, way, length - 1).wait_recv()
                result = result + in_buf[t, base + length - 1].astype(F32)
        if s == half:
            out_ref[:, t * cols : (t + 1) * cols] = result.astype(BF16)

    for s in range(half + 1):
        for t in range(TILES):
            stage(t, s)
    for t in range(TILES):
        for way in (0, 1):
            for s in range(hops(t)[way]):
                move(t, way, s).wait_send()

    for kind in range(12):
        cond, copy = sends[kind]

        @pl.when(cond)
        def _(copy=copy):
            copy.wait_send()

        _, read, slot, _ = arrivals[kind]

        @pl.when(read)
        def _(slot=slot):
            relay(slot).wait_send()

    @pl.when(core == 0)
    def _():
        own_to_partner.wait_send()
    each(lambda i: give(*kv_rows, i).wait_send())
    each(lambda i: give(*q_rows, i).wait_send())


def per_device(
    queries, keys, values, cf_queries, cf_keys, cf_values, patch_source, doc_lengths, out_weight
):
    ctx = lax.axis_size("ctx")
    groups = lax.axis_size("head")
    wide = queries.shape[1]
    heads = wide // HD
    feats = out_weight.shape[1]
    share, cols = ROWS // groups, feats // TILES
    dma = pltpu.SemaphoreType.DMA
    return pl.pallas_call(
        layer_kernel,
        name="layer",
        out_shape=jax.ShapeDtypeStruct((share, feats), BF16),
        in_specs=[VMEM] * 8 + [ANY],
        out_specs=VMEM,
        scratch_shapes=[
            pltpu.VMEM((ctx, SLOT, 2 * HD), BF16),
            pltpu.VMEM((ctx, SLOT, 2 * HD), BF16),
            pltpu.VMEM((ctx, SLOT, wide), BF16),
            pltpu.VMEM((ctx, SLOT, wide), BF16),
            pltpu.VMEM((2, ROWS, HD), BF16),
            pltpu.VMEM((heads, ROWS, 2 * HD), BF16),
            pltpu.VMEM((4 * SIDE, 2, 2, ROWS, 2 * HD), BF16),
            pltpu.VMEM((heads, ROWS, HD), F32),
            pltpu.VMEM((heads, ROWS, HD), F32),
            pltpu.VMEM((heads, ROWS, HD), F32),
            pltpu.VMEM((ROWS, wide), BF16),
            pltpu.VMEM((TILES, wide, cols), BF16),
            pltpu.VMEM((TILES, groups, share, cols), F32),
            pltpu.VMEM((TILES, groups - 1, share, cols), BF16),
            pltpu.VMEM((TILES, groups - 1, share, cols), BF16),
            dma((ctx,)),
            dma((ctx,)),
            dma((ctx,)),
            dma((ctx,)),
            dma((12,)),
            dma((12,)),
            dma((4 * SIDE,)),
            dma((4 * SIDE,)),
            dma((TILES,)),
            dma((TILES, groups - 1)),
            dma((TILES, groups - 1)),
        ],
        compiler_params=pltpu.CompilerParams(collective_id=0, has_side_effects=True),
    )(
        patch_source.reshape(2 * ctx, BLK), doc_lengths.reshape(1, -1),
        queries, keys, values, cf_queries, cf_keys, cf_values, out_weight,
    )


def solution(mesh):
    in_specs = (
        P("ctx", "head"),
        P("ctx", "head"),
        P("ctx", "head"),
        P("ctx", "head"),
        P("ctx", "head"),
        P("ctx", "head"),
        P(),
        P(),
        P("head", None),
    )
    out_specs = P(("ctx", "head"), None)
    return jax.shard_map(
        per_device, mesh=mesh, in_specs=in_specs, out_specs=out_specs, check_vma=False
    )
```

time: 86.3 us -> 75.4 us (0.87)
  the two profiles are of different devices: /device:TPU:7 before, /device:TPU:5 now
where the time goes in v4:
time: 75.4 us; the launch traced here: 75.3 us
  Pallas kernels  73.6 us (98%)
  local copies, waits for them, and re-layouts  1.67 us (2%)
    pallas_call x1, Pallas kernels, per_device(): pl.pallas_call(layer_kernel, name='layer', out_shape=jax.ShapeDtypeStruct...  73.6 us
    unnamed x1, local copies, waits for them, and re-layouts  1.67 us

profile of v4, /device:TPU:5, one launch (start us, length us, event | category | flops | bytes accessed | tf_op | source)
XLA Modules:
  0.0 75.3 jit_solution(6357831556594996718)
XLA Ops:
  0.0 73.6 %layer.1 = bf16[32,4096]{1,0:T(8,128)(2,1)} custom-call(s32[64,128]{1,0:T(8,128)} %bitcast.2, s32[1,32]{1,0:T(1,128)} %bitcast.3, bf16[256,1024]{1,0:T(8,128)(2,1)} %q_ref.1, bf16[256,128]{1,0:T(8,128)(2,1)} %k_ref.1, bf16[256,128]{1,0:T(8,128)(2,1)} %v_ref.1, bf16[256,1024]{1,0:T(8,128)(2,1)} %cq_ref.1, bf16[256,128]{1,0:T(8,128)(2,1)} %ck_ref.1, ...), custom_call_target="tpu_custom_call" | custom-call | tf_op jit(solution)/shard_map/layer/pallas_call | solution.py:490
  73.6 1.7 %copy.11 = bf16[32,4096]{1,0:T(8,128)(2,1)} copy(bf16[32,4096]{1,0:T(8,128)(2,1)} %layer.1) | data formatting | bytes 524288
